TPU v7x, 32 devices: a whole 2x2x4 slice. The times are simulated.
32 devices in a mesh: row: 4 (over z), col: 8 (over y, x, core).
Axes of the slice: x: 2, y: 2, z: 4, core: 2. Of those that a mesh axis runs over, the one named last changes fastest.
Arguments:
- parent_rhs: bfloat16 [12288, 128], P('row'), may hold values from -6 to 6
- parent_inverse: bfloat16 [48, 256, 256], P('row')
- parent_left: bfloat16 [48, 48, 128, 256], P('row', 'col'), may hold values from -0.0546875 to 0.0546875
- parent_right: bfloat16 [48, 48, 128, 256], P('row', 'col'), may hold values from -0.375 to 0.375
- parent_ranks: int32 [48, 48], P('row', 'col'), may hold values from 1 to 128, as said below
- parent_slots: int32 [48], P('col'), may hold values from 0 to 47, each once
- inner_left: bfloat16 [8, 15, 128, 256], P('row'), may hold values from -0.0546875 to 0.0546875
- inner_right: bfloat16 [8, 15, 128, 256], P('row'), may hold values from -0.375 to 0.375
- inner_ranks: int32 [8, 15], P('row'), may hold values from 1 to 128
- child_rhs: bfloat16 [8192, 128], P('row'), may hold values from -6 to 6
- child_inverse: bfloat16 [32, 256, 256], P('row')
- child_left: bfloat16 [32, 16, 128, 256], P('row', 'col'), may hold values from -0.09375 to 0.09375
- child_right: bfloat16 [32, 16, 128, 256], P('row', 'col'), may hold values from -0.375 to 0.375
- child_ranks: int32 [32, 16], P('row', 'col'), may hold values from 1 to 128
- child_slots: int32 [2, 16], P(None, 'col'), may hold values from 0 to 15, each once within a row
- child_inner_left: bfloat16 [8, 6, 128, 256], P('row'), may hold values from -0.09375 to 0.09375
- child_inner_right: bfloat16 [8, 6, 128, 256], P('row'), may hold values from -0.375 to 0.375
- child_inner_ranks: int32 [8, 6], P('row'), may hold values from 1 to 128
- border_left: bfloat16 [32, 16, 128, 256], P('row', 'col'), may hold values from -0.1875 to 0.1875
- border_right: bfloat16 [32, 16, 128, 256], P('row', 'col'), may hold values from -0.375 to 0.375
- border_ranks: int32 [32, 16], P('row', 'col'), may hold values from 1 to 128
- border_map: int32 [32], P('row'), may hold values from 0 to 47, as said below
Outputs:
- child_solution: bfloat16 [8192, 128], P('row')
- parent_solution: bfloat16 [12288, 128], P('row')
Inputs may be any that keep to these rules, and one draw needn't show every extreme that they name: `parent_ranks`: only the leading rows of a tile's factors up to its rank are used. `border_map`: within one child's 16 border rows no parent tile row repeats; the two children may share parent tile rows. `parent_slots`: each tile column appears in exactly one slot. `child_slots`: for each child, each tile column appears in exactly one slot.
All inputs are finite; a program needn't handle non-finite values.
Results may differ from a plain program's by a relative error of at most 0.018.
Values may be sent and summed in bfloat16 or wider, within the bound.
A program may use at most 128 MiB of HBM per device.

v0:
```python
import jax
import jax.numpy as jnp
from jax import lax
from jax.sharding import PartitionSpec as P

PT = 48
GP = 6
GC = 4
NSBP = 8
NSBC = 4


def shortened(value):

    def short(part):
        return part.astype(jnp.bfloat16) if part.dtype == jnp.float32 else part

    return jax.tree.map(short, value)


def swapped(value, axis, apart):
    mask = 2**apart
    pairs = [(source, source ^ mask) for source in range(lax.axis_size(axis))]
    return lax.ppermute(value, axis, pairs)


def from_root(value, axis, source):
    kept = jnp.where(lax.axis_index(axis) == source, value, 0).astype(value.dtype)
    return lax.psum(kept, axis)


def masked_cast(values, keep_mask):
    return jnp.where(keep_mask, values, 0.0).astype(jnp.bfloat16)


def solve_block(right_side, far_part, inverse, near_left, near_right, near_ranks, group_size):
    rank_iota = jnp.arange(near_left.shape[1])
    solved = []
    for position in range(group_size):
        running_sum = right_side[position] - far_part[position]
        if position > 0:
            first_pair = position * (position - 1) // 2
            earlier = jnp.stack(solved)
            left_part = near_left[first_pair : first_pair + position]
            right_part = near_right[first_pair : first_pair + position]
            ranks_part = near_ranks[first_pair : first_pair + position]
            coeffs = jnp.einsum(
                "mrt,mtn->mrn", right_part, earlier, preferred_element_type=jnp.float32
            )
            coeffs = masked_cast(coeffs, (rank_iota[None, :] < ranks_part[:, None])[:, :, None])
            running_sum = running_sum - jnp.einsum(
                "mrt,mrn->tn", left_part, coeffs, preferred_element_type=jnp.float32
            )
        residue = running_sum.astype(jnp.bfloat16)
        solved.append(
            jnp.dot(inverse[position], residue, preferred_element_type=jnp.float32).astype(
                jnp.bfloat16
            )
        )
    return jnp.stack(solved)


def far_block(left_factor, right_factor, tile_ranks, known_tiles, usable):
    coeffs = jnp.einsum(
        "gkrt,ktn->gkrn", right_factor, known_tiles, preferred_element_type=jnp.float32
    )
    rank_iota = jnp.arange(left_factor.shape[2])
    keep_mask = (rank_iota[None, None, :] < tile_ranks[:, :, None]) & usable[None, :, None]
    coeffs = masked_cast(coeffs, keep_mask[..., None])
    return jnp.einsum("gkrt,gkrn->gtn", left_factor, coeffs, preferred_element_type=jnp.float32)


def column_sum(partial_value):
    return lax.psum(partial_value.astype(jnp.bfloat16), "col").astype(jnp.float32)


def spread_half(values, half_bits):
    spread = values
    for bit_number in range(half_bits):
        spread = spread + swapped(shortened(spread), "row", bit_number).astype(spread.dtype)
    return spread


def on_device(
    parent_rhs,
    parent_inverse,
    parent_left,
    parent_right,
    parent_ranks,
    parent_slots,
    inner_left,
    inner_right,
    inner_ranks,
    child_rhs,
    child_inverse,
    child_left,
    child_right,
    child_ranks,
    child_slots,
    child_inner_left,
    child_inner_right,
    child_inner_ranks,
    border_left,
    border_right,
    border_ranks,
    border_map,
):
    tile_size = parent_inverse.shape[1]
    columns = parent_rhs.shape[1]
    row_index = lax.axis_index("row")
    row_count = lax.axis_size("row")
    half_rows = row_count // 2
    half_bits = half_rows.bit_length() - 1
    child_index = row_index // half_rows
    child_place = row_index % half_rows
    child_tiles = child_inverse.shape[0]
    child_blocks = child_tiles // GC
    my_columns = lax.dynamic_index_in_dim(child_slots, child_index, 0, keepdims=False)
    column_block = my_columns // GC
    child_side = child_rhs.reshape(child_tiles, tile_size, columns).astype(jnp.float32)
    slot_count = my_columns.shape[0]
    known_tiles = jnp.zeros((slot_count, tile_size, columns), jnp.bfloat16)
    child_solved = jnp.zeros((child_tiles, tile_size, columns), jnp.bfloat16)
    child_empty = jnp.zeros((GC, tile_size, columns), jnp.float32)
    child_blank = jnp.zeros((GC, tile_size, columns), jnp.bfloat16)
    for step_index in range(NSBC):
        owner_place = step_index // child_blocks
        local_block = step_index % child_blocks
        is_owner = child_place == owner_place
        lower = local_block * GC
        upper = lower + GC
        partial_value = lax.cond(
            is_owner,
            lambda: far_block(
                child_left[lower:upper],
                child_right[lower:upper],
                child_ranks[lower:upper],
                known_tiles,
                column_block < step_index,
            ),
            lambda: child_empty,
        )
        far_part = column_sum(partial_value)
        new_tiles = lax.cond(
            is_owner,
            lambda: solve_block(
                child_side[lower:upper],
                far_part,
                child_inverse[lower:upper],
                child_inner_left[local_block],
                child_inner_right[local_block],
                child_inner_ranks[local_block],
                GC,
            ),
            lambda: child_blank,
        )
        child_solved = child_solved.at[lower:upper].set(
            jnp.where(is_owner, new_tiles, child_solved[lower:upper])
        )
        slot_tiles = jnp.take(new_tiles, jnp.clip(my_columns - step_index * GC, 0, GC - 1), axis=0)
        from_owner = spread_half(slot_tiles, half_bits)
        known_tiles = jnp.where(
            (column_block == step_index)[:, None, None], from_owner, known_tiles
        )
    rank_iota = jnp.arange(border_left.shape[2])
    coeffs = jnp.einsum(
        "kjrt,jtn->kjrn", border_right, known_tiles, preferred_element_type=jnp.float32
    )
    coeffs = masked_cast(coeffs, (rank_iota[None, None, :] < border_ranks[:, :, None])[..., None])
    border_part = -jnp.einsum(
        "kjrt,kjrn->ktn", border_left, coeffs, preferred_element_type=jnp.float32
    )
    parent_tiles = parent_inverse.shape[0]
    target = (border_map[:, None] == jnp.arange(PT)[None, :]).astype(jnp.float32)
    dense = jnp.einsum("kp,ktn->ptn", target, border_part, precision=lax.Precision.HIGHEST).reshape(
        PT * tile_size, columns
    )
    share = lax.psum_scatter(dense, ("row", "col"), scatter_dimension=0, tiled=True)
    extension = (
        lax.all_gather(share.astype(jnp.bfloat16), "col", axis=0, tiled=True)
        .astype(share.dtype)
        .reshape(parent_tiles, tile_size, columns)
    )
    parent_side = (
        parent_rhs.reshape(parent_tiles, tile_size, columns).astype(jnp.float32) + extension
    )
    parent_blocks = parent_tiles // GP
    parent_block_of = parent_slots // GP
    parent_count = parent_slots.shape[0]
    known_parent = jnp.zeros((parent_count, tile_size, columns), jnp.bfloat16)
    parent_solved = jnp.zeros((parent_tiles, tile_size, columns), jnp.bfloat16)
    parent_empty = jnp.zeros((GP, tile_size, columns), jnp.float32)
    parent_blank = jnp.zeros((GP, tile_size, columns), jnp.bfloat16)
    for step_index in range(NSBP):
        owner_row = step_index // parent_blocks
        local_block = step_index % parent_blocks
        is_owner = row_index == owner_row
        lower = local_block * GP
        upper = lower + GP
        partial_value = lax.cond(
            is_owner,
            lambda: far_block(
                parent_left[lower:upper],
                parent_right[lower:upper],
                parent_ranks[lower:upper],
                known_parent,
                parent_block_of < step_index,
            ),
            lambda: parent_empty,
        )
        far_part = column_sum(partial_value)
        new_tiles = lax.cond(
            is_owner,
            lambda: solve_block(
                parent_side[lower:upper],
                far_part,
                parent_inverse[lower:upper],
                inner_left[local_block],
                inner_right[local_block],
                inner_ranks[local_block],
                GP,
            ),
            lambda: parent_blank,
        )
        parent_solved = parent_solved.at[lower:upper].set(
            jnp.where(is_owner, new_tiles, parent_solved[lower:upper])
        )
        if step_index + 1 < NSBP:
            slot_tiles = jnp.take(
                new_tiles, jnp.clip(parent_slots - step_index * GP, 0, GP - 1), axis=0
            )
            arrived = from_root(shortened(slot_tiles), "row", owner_row).astype(slot_tiles.dtype)
            fresh_mask = parent_block_of == step_index
            known_parent = jnp.where(fresh_mask[:, None, None], arrived, known_parent)
    child_solution = child_solved.reshape(child_tiles * tile_size, columns)
    parent_solution = parent_solved.reshape(parent_tiles * tile_size, columns)
    return (child_solution, parent_solution)


def solution(mesh):
    placed = (
        P("row", None),
        P("row", None, None),
        P("row", "col", None, None),
        P("row", "col", None, None),
        P("row", "col"),
        P("col"),
        P("row", None, None, None),
        P("row", None, None, None),
        P("row", None),
        P("row", None),
        P("row", None, None),
        P("row", "col", None, None),
        P("row", "col", None, None),
        P("row", "col"),
        P(None, "col"),
        P("row", None, None, None),
        P("row", None, None, None),
        P("row", None),
        P("row", "col", None, None),
        P("row", "col", None, None),
        P("row", "col"),
        P("row"),
    )
    return jax.shard_map(
        on_device,
        mesh=mesh,
        in_specs=placed,
        out_specs=(P("row", None), P("row", None)),
        check_vma=False,
    )
```

profile of v0, /device:TPU:25, one launch (start us, length us, event | category | flops | bytes accessed | tf_op | source)
XLA Modules:
  0.0 1329.8 jit_solution(8931553234851429683)
XLA Ops:
  11.3 54.4 %all-reduce.20.cloned.1.call-done = bf16[4,256,128]{2,1,0:T(8,128)(2,1)} async-done(((bf16[4,256,128]{2,1,0:T(8,128)(2,1)}), bf16[4,256,128]{2,1,0:T(8,128)(2,1)}) %all-reduce.20.cloned.1.call-update) | async-done | bytes 262160 | tf_op jit(solution)/shard_map/psum | solution.py:74
  66.4 9.6 collective-permute-start
  76.5 1.8 collective-permute-done
  79.4 56.7 %all-reduce.22.cloned.1.call-done = bf16[4,256,128]{2,1,0:T(8,128)(2,1)} async-done(((bf16[4,256,128]{2,1,0:T(8,128)(2,1)}), bf16[4,256,128]{2,1,0:T(8,128)(2,1)}) %all-reduce.22.cloned.1.call-update) | async-done | bytes 262160 | tf_op jit(solution)/shard_map/psum | solution.py:74
  136.8 9.6 collective-permute-start.1
  146.4 2.4 collective-permute-done.1
  149.5 1.9 conditional.28
  152.3 54.2 %all-reduce.24.cloned.1.call-done = bf16[4,256,128]{2,1,0:T(8,128)(2,1)} async-done(((bf16[4,256,128]{2,1,0:T(8,128)(2,1)}), bf16[4,256,128]{2,1,0:T(8,128)(2,1)}) %all-reduce.24.cloned.1.call-update) | async-done | bytes 262160 | tf_op jit(solution)/shard_map/psum | solution.py:74
  206.6 11.4 conditional.29
  223.7 2.5 conditional.30
  227.3 55.9 %all-reduce.54.cloned.1.call-done = (bf16[4,256,128]{2,1,0:T(8,128)(2,1)}, bf16[6,256,128]{2,1,0:T(8,128)(2,1)}) async-done(((bf16[4,256,128]{2,1,0:T(8,128)(2,1)}, bf16[6,256,128]{2,1,0:T(8,128)(2,1)}), (bf16[4,256,128]{2,1,0:T(8,128)(2,1)}, bf16[6,256,128]{2,1,0:T(8,128)(2,1)})) %all-reduce.54.cloned.1.call-update) | async-done | bytes 655376 | tf_op jit(solution)/shard_map/psum | solution.py:74
  283.1 9.8 conditional.31
  293.8 3.7 collective-permute-done.3
  297.5 2.0 fusion.1506
  299.9 2.7 fusion.1507
  302.7 4.6 copy.75
  307.8 113.1 %reduce-scatter.2.cloned.1.call-done = f32[384,128]{1,0:T(8,128)} async-done(((f32[12288,128]{1,0:T(8,128)}), f32[384,128]{1,0:T(8,128)}) %reduce-scatter.2.cloned.1.call-update) | async-done | bytes 196624 | tf_op jit(solution)/shard_map/reduce_scatter | solution.py:178
  421.8 12.7 all_gather.3
  436.8 2.3 gather_fusion.4
  439.1 1.9 select_select_fusion.6
  441.6 53.6 %all-reduce.26.cloned.1.call-done = bf16[6,256,128]{1,2,0:T(8,128)(2,1)} async-done(((bf16[6,256,128]{1,2,0:T(8,128)(2,1)}), bf16[6,256,128]{1,2,0:T(8,128)(2,1)}) %all-reduce.26.cloned.1.call-update) | async-done | bytes 393232 | tf_op jit(solution)/shard_map/psum | solution.py:29
  495.2 1.8 broadcast_select_fusion.5
  497.8 1.9 copy.80
  499.8 58.9 %all-reduce.28.cloned.1.call-done = bf16[6,256,128]{2,1,0:T(8,128)(2,1)} async-done(((bf16[6,256,128]{2,1,0:T(8,128)(2,1)}), bf16[6,256,128]{2,1,0:T(8,128)(2,1)}) %all-reduce.28.cloned.1.call-update) | async-done | bytes 393232 | tf_op jit(solution)/shard_map/psum | solution.py:74
  559.6 2.3 gather_fusion.5
  562.0 1.9 select_select_fusion.5
  563.9 53.6 %all-reduce.30.cloned.1.call-done = bf16[6,256,128]{1,2,0:T(8,128)(2,1)} async-done(((bf16[6,256,128]{1,2,0:T(8,128)(2,1)}), bf16[6,256,128]{1,2,0:T(8,128)(2,1)}) %all-reduce.30.cloned.1.call-update) | async-done | bytes 393232 | tf_op jit(solution)/shard_map/psum | solution.py:29
  617.5 2.0 broadcast_select_fusion.4
  620.3 1.9 copy.83
  622.3 59.8 %all-reduce.32.cloned.1.call-done = bf16[6,256,128]{2,1,0:T(8,128)(2,1)} async-done(((bf16[6,256,128]{2,1,0:T(8,128)(2,1)}), bf16[6,256,128]{2,1,0:T(8,128)(2,1)}) %all-reduce.32.cloned.1.call-update) | async-done | bytes 393232 | tf_op jit(solution)/shard_map/psum | solution.py:74
  682.9 2.3 gather_fusion.6
  685.2 1.9 select_select_fusion.4
  687.1 54.6 %all-reduce.34.cloned.1.call-done = bf16[6,256,128]{1,2,0:T(8,128)(2,1)} async-done(((bf16[6,256,128]{1,2,0:T(8,128)(2,1)}), bf16[6,256,128]{1,2,0:T(8,128)(2,1)}) %all-reduce.34.cloned.1.call-update) | async-done | bytes 393232 | tf_op jit(solution)/shard_map/psum | solution.py:29
  741.7 2.0 broadcast_select_fusion.3
  744.5 1.9 copy.86
  747.1 59.2 %all-reduce.36.cloned.1.call-done = bf16[6,256,128]{2,1,0:T(8,128)(2,1)} async-done(((bf16[6,256,128]{2,1,0:T(8,128)(2,1)}), bf16[6,256,128]{2,1,0:T(8,128)(2,1)}) %all-reduce.36.cloned.1.call-update) | async-done | bytes 393232 | tf_op jit(solution)/shard_map/psum | solution.py:74
  807.1 2.3 gather_fusion.7
  809.4 1.9 select_select_fusion.3
  812.1 53.8 %all-reduce.38.cloned.1.call-done = bf16[6,256,128]{1,2,0:T(8,128)(2,1)} async-done(((bf16[6,256,128]{1,2,0:T(8,128)(2,1)}), bf16[6,256,128]{1,2,0:T(8,128)(2,1)}) %all-reduce.38.cloned.1.call-update) | async-done | bytes 393232 | tf_op jit(solution)/shard_map/psum | solution.py:29
  866.0 2.0 broadcast_select_fusion.2
  868.7 1.9 copy.89
  870.8 1.8 pad_maximum_fusion.5
  872.6 58.7 %all-reduce.40.cloned.1.call-done = bf16[6,256,128]{2,1,0:T(8,128)(2,1)} async-done(((bf16[6,256,128]{2,1,0:T(8,128)(2,1)}), bf16[6,256,128]{2,1,0:T(8,128)(2,1)}) %all-reduce.40.cloned.1.call-update) | async-done | bytes 393232 | tf_op jit(solution)/shard_map/psum | solution.py:74
  932.3 2.4 gather_fusion.8
  934.7 1.9 select_select_fusion.2
  936.7 1.7 select_dynamic-update-slice_fusion.1
  938.4 1.9 fusion.1516
  940.3 2.0 copy.73
  942.3 50.0 %all-reduce.42.cloned.1.call-done = bf16[6,256,128]{1,2,0:T(8,128)(2,1)} async-done(((bf16[6,256,128]{1,2,0:T(8,128)(2,1)}), bf16[6,256,128]{1,2,0:T(8,128)(2,1)}) %all-reduce.42.cloned.1.call-update) | async-done | bytes 393232 | tf_op jit(solution)/shard_map/psum | solution.py:29
  992.3 1.9 broadcast_select_fusion.1
  995.2 61.1 %all-reduce.44.cloned.1.call-done = bf16[6,256,128]{2,1,0:T(8,128)(2,1)} async-done(((bf16[6,256,128]{2,1,0:T(8,128)(2,1)}), bf16[6,256,128]{2,1,0:T(8,128)(2,1)}) %all-reduce.44.cloned.1.call-update) | async-done | bytes 393232 | tf_op jit(solution)/shard_map/psum | solution.py:74
  1060.6 61.6 %all-reduce.46.cloned.1.call-done = bf16[6,256,128]{1,2,0:T(8,128)(2,1)} async-done(((bf16[6,256,128]{1,2,0:T(8,128)(2,1)}), bf16[6,256,128]{1,2,0:T(8,128)(2,1)}) %all-reduce.46.cloned.1.call-update) | async-done | bytes 393232 | tf_op jit(solution)/shard_map/psum | solution.py:29
  1123.3 3.8 conditional.44
  1123.5 3.6 fusion.1217
  1128.3 56.5 %all-reduce.48.cloned.1.call-done = bf16[6,256,128]{2,1,0:T(8,128)(2,1)} async-done(((bf16[6,256,128]{2,1,0:T(8,128)(2,1)}), bf16[6,256,128]{2,1,0:T(8,128)(2,1)}) %all-reduce.48.cloned.1.call-update) | async-done | bytes 393232 | tf_op jit(solution)/shard_map/psum | solution.py:74
  1184.8 18.0 %conditional.45 = (bf16[6,256,128]{1,2,0:T(8,128)(2,1)}) conditional(s32[]{:T(128)} %convert_element_type.1117, () %tuple.242, (f32[12,256,128]{2,1,0:T(8,128)}, bf16[6,256,128]{2,1,0:T(8,128)(2,1)}, bf16[12,256,256]{2,1,0:T(8,128)(2,1)S(1)}, s32[2,15]{1,0:T(2,128)S(1)}, bf16[2,15,128,256]{3,2,1,0:T(8,128)(2,1)}, ...), branch_computations={%region_60.63_spmd, %region_61.64_spmd} | conditional | flops 354420608 | bytes 11210712 | solution.py:212
  1190.7 2.0 constant_dynamic-update-slice_fusion.63
  1205.7 33.6 %all-reduce.50.cloned.1.call-done = bf16[6,256,128]{1,2,0:T(8,128)(2,1)} async-done(((bf16[6,256,128]{1,2,0:T(8,128)(2,1)}), bf16[6,256,128]{1,2,0:T(8,128)(2,1)}) %all-reduce.50.cloned.1.call-update) | async-done | bytes 393232 | tf_op jit(solution)/shard_map/psum | solution.py:29
  1239.2 6.6 conditional.46
  1241.6 4.0 fusion.1362
  1248.0 55.6 %all-reduce.52.cloned.1.call-done = bf16[6,256,128]{2,1,0:T(8,128)(2,1)} async-done(((bf16[6,256,128]{2,1,0:T(8,128)(2,1)}), bf16[6,256,128]{2,1,0:T(8,128)(2,1)}) %all-reduce.52.cloned.1.call-update) | async-done | bytes 393232 | tf_op jit(solution)/shard_map/psum | solution.py:74
  1303.5 17.1 %conditional.47 = (bf16[6,256,128]{1,2,0:T(8,128)(2,1)}) conditional(s32[]{:T(128)} %convert_element_type.1117, () %tuple.246, (f32[12,256,128]{2,1,0:T(8,128)}, bf16[6,256,128]{2,1,0:T(8,128)(2,1)}, bf16[12,256,256]{2,1,0:T(8,128)(2,1)S(1)}, s32[2,15]{1,0:T(2,128)S(1)}, bf16[2,15,128,256]{3,2,1,0:T(8,128)(2,1)}, ...), branch_computations={%region_66.69_spmd, %region_67.70_spmd} | conditional | flops 354420608 | bytes 8064956 | solution.py:212
  1304.6 1.8 constant_dynamic-update-slice_fusion.74
  1308.5 2.0 constant_dynamic-update-slice_fusion.73
  (314 shorter events, 108.8 us)
Async XLA Ops:
  7.2 290.4 %copy-start = (bf16[8,2,128,256]{3,2,1,0:T(8,128)(2,1)S(1)}, bf16[8,2,128,256]{3,2,1,0:T(8,128)(2,1)}, u32[]{:S(2)}) copy-start(bf16[8,2,128,256]{3,2,1,0:T(8,128)(2,1)} %param.116) | copy-start | bytes 3145732
  7.2 3.0 copy-start.17
  7.2 58.5 %all-reduce.20.cloned.1.call-start = ((), (), s32[]{:S(2)}) async-start(), calls=%async_computation.1 | async-start | bytes 524288 | tf_op jit(solution)/shard_map/psum | solution.py:74
  8.6 140.9 %copy-start.45 = (s32[2]{0:T(128)}, s32[2]{0:T(128)S(1)}, u32[]{:S(2)}) copy-start(s32[2]{0:T(128)S(1)} %get-tuple-element.770) | copy-start | bytes 28
  8.6 57.0 %copy-start.4 = (bf16[8,256,256]{2,1,0:T(8,128)(2,1)S(1)}, bf16[8,256,256]{2,1,0:T(8,128)(2,1)}, u32[]{:S(2)}) copy-start(bf16[8,256,256]{2,1,0:T(8,128)(2,1)} %param.108) | copy-start | bytes 3145732
  8.6 57.0 %copy-start.48 = (s32[2,6]{1,0:T(2,128)S(1)}, s32[2,6]{1,0:T(2,128)}, u32[]{:S(2)}) copy-start(s32[2,6]{1,0:T(2,128)} %param.115) | copy-start | bytes 148
  9.5 126.6 %all-reduce.22.cloned.1.call-start = ((), (), s32[]{:S(2)}) async-start(), calls=%async_computation.2 | async-start | bytes 524288 | tf_op jit(solution)/shard_map/psum | solution.py:74
  65.7 12.7 copy-start.26
  66.4 12.0 collective-permute-start
  79.4 127.2 %all-reduce.24.cloned.1.call-start = ((), (), s32[]{:S(2)}) async-start(), calls=%async_computation.3 | async-start | bytes 524288 | tf_op jit(solution)/shard_map/psum | solution.py:74
  136.1 83.9 %copy-start.5 = (bf16[4,256,128]{1,2,0:T(8,128)(2,1)}, bf16[4,256,128]{1,2,0:T(8,128)(2,1)S(1)}, u32[]{:S(2)}) copy-start(bf16[4,256,128]{1,2,0:T(8,128)(2,1)S(1)} %get-tuple-element.927) | copy-start | bytes 786436
  136.8 12.0 collective-permute-start.1
  152.3 130.9 %all-reduce.54.cloned.1.call-start = ((), (), s32[]{:S(2)}) async-start(), calls=%async_computation.19 | async-start | bytes 1310720 | tf_op jit(solution)/shard_map/psum | solution.py:74
  206.6 13.5 %copy-start.18 = (s32[12,6]{0,1:T(8,128)S(1)}, s32[12,6]{0,1:T(8,128)}, u32[]{:S(2)}) copy-start(s32[12,6]{0,1:T(8,128)} %param.102) | copy-start | bytes 868
  206.6 2.6 copy-start.50
  218.7 4.0 collective-permute-start.2
  221.0 6.2 copy-start.46
  221.0 6.3 copy-start.42
  221.0 62.1 %copy-start.49 = (s32[2,6]{1,0:T(2,128)S(1)}, s32[2,6]{1,0:T(2,128)}, u32[]{:S(2)}) copy-start(s32[2,6]{1,0:T(2,128)} %param.115) | copy-start | bytes 148
  227.1 193.8 %reduce-scatter.2.cloned.1.call-start = ((), (), s32[]{:S(2)}) async-start(), calls=%async_computation.4 | async-start | bytes 6488064 | tf_op jit(solution)/shard_map/reduce_scatter | solution.py:178
  283.1 10.4 copy-start.32
  283.1 14.4 %copy-start.31 = (pred[2]{0:T(512)(128)(4,1)S(1)}, pred[2]{0:T(512)(128)(4,1)}, u32[]{:S(2)}) copy-start(pred[2]{0:T(512)(128)(4,1)} %get-tuple-element.769) | copy-start | bytes 10
  293.0 6.5 copy-start.7
  293.6 3.9 collective-permute-start.3
  307.2 188.0 %all-reduce.26.cloned.1.call-start = ((), (), s32[]{:S(2)}) async-start(), calls=%async_computation.5 | async-start | bytes 786432 | tf_op jit(solution)/shard_map/psum | solution.py:29
  421.8 14.0 %copy-start.2 = (bf16[12,256,256]{2,1,0:T(8,128)(2,1)S(1)}, bf16[12,256,256]{2,1,0:T(8,128)(2,1)}, u32[]{:S(2)}) copy-start(bf16[12,256,256]{2,1,0:T(8,128)(2,1)} %param.99) | copy-start | bytes 4718596
  421.8 14.0 %copy-start.51 = (s32[2,15]{1,0:T(2,128)S(1)}, s32[2,15]{1,0:T(2,128)}, u32[]{:S(2)}) copy-start(s32[2,15]{1,0:T(2,128)} %param.106) | copy-start | bytes 364
  435.8 620.6 %copy-start.3 = (f32[3072,128]{1,0:T(8,128)}, f32[3072,128]{1,0:T(8,128)S(1)}, u32[]{:S(2)}) copy-start(f32[3072,128]{1,0:T(8,128)S(1)} %convert_add_fusion) | copy-start | bytes 4718596
  435.8 3.3 copy-start.33
  441.0 117.7 %all-reduce.28.cloned.1.call-start = ((), (), s32[]{:S(2)}) async-start(), calls=%async_computation.6 | async-start | bytes 786432 | tf_op jit(solution)/shard_map/psum | solution.py:74
  497.0 2.8 copy-start.43
  497.1 61.6 %copy-start.52 = (s32[2,15]{1,0:T(2,128)S(1)}, s32[2,15]{1,0:T(2,128)}, u32[]{:S(2)}) copy-start(s32[2,15]{1,0:T(2,128)} %param.106) | copy-start | bytes 364
  499.8 117.8 %all-reduce.30.cloned.1.call-start = ((), (), s32[]{:S(2)}) async-start(), calls=%async_computation.7 | async-start | bytes 786432 | tf_op jit(solution)/shard_map/psum | solution.py:29
  559.6 57.9 %copy-start.36 = (pred[6]{0:T(512)(128)(4,1)S(1)}, pred[6]{0:T(512)(128)(4,1)}, u32[]{:S(2)}) copy-start(pred[6]{0:T(512)(128)(4,1)} %get-tuple-element.911) | copy-start | bytes 22
  563.8 118.2 %all-reduce.32.cloned.1.call-start = ((), (), s32[]{:S(2)}) async-start(), calls=%async_computation.8 | async-start | bytes 786432 | tf_op jit(solution)/shard_map/psum | solution.py:74
  619.5 2.8 copy-start.41
  619.5 62.6 %copy-start.53 = (s32[2,15]{1,0:T(2,128)S(1)}, s32[2,15]{1,0:T(2,128)}, u32[]{:S(2)}) copy-start(s32[2,15]{1,0:T(2,128)} %param.106) | copy-start | bytes 364
  622.2 119.5 %all-reduce.34.cloned.1.call-start = ((), (), s32[]{:S(2)}) async-start(), calls=%async_computation.9 | async-start | bytes 786432 | tf_op jit(solution)/shard_map/psum | solution.py:29
  682.1 3.1 copy-start.30
  682.9 58.9 %copy-start.35 = (pred[6]{0:T(512)(128)(4,1)S(1)}, pred[6]{0:T(512)(128)(4,1)}, u32[]{:S(2)}) copy-start(pred[6]{0:T(512)(128)(4,1)} %get-tuple-element.910) | copy-start | bytes 22
  687.1 119.2 %all-reduce.36.cloned.1.call-start = ((), (), s32[]{:S(2)}) async-start(), calls=%async_computation.10 | async-start | bytes 786432 | tf_op jit(solution)/shard_map/psum | solution.py:74
  743.7 2.8 copy-start.40
  743.7 2.8 copy-start.39
  743.7 62.6 %copy-start.54 = (s32[2,15]{1,0:T(2,128)S(1)}, s32[2,15]{1,0:T(2,128)}, u32[]{:S(2)}) copy-start(s32[2,15]{1,0:T(2,128)} %param.106) | copy-start | bytes 364
  746.4 119.6 %all-reduce.38.cloned.1.call-start = ((), (), s32[]{:S(2)}) async-start(), calls=%async_computation.11 | async-start | bytes 786432 | tf_op jit(solution)/shard_map/psum | solution.py:29
  806.3 3.1 copy-start.29
  807.1 4.3 copy-start.38
  807.1 4.3 copy-start.37
  807.1 58.9 %copy-start.34 = (pred[6]{0:T(512)(128)(4,1)S(1)}, pred[6]{0:T(512)(128)(4,1)}, u32[]{:S(2)}) copy-start(pred[6]{0:T(512)(128)(4,1)} %get-tuple-element.909) | copy-start | bytes 22
  811.3 120.0 %all-reduce.40.cloned.1.call-start = ((), (), s32[]{:S(2)}) async-start(), calls=%async_computation.12 | async-start | bytes 786432 | tf_op jit(solution)/shard_map/psum | solution.py:74
  868.7 62.6 %copy-start.55 = (s32[2,15]{1,0:T(2,128)S(1)}, s32[2,15]{1,0:T(2,128)}, u32[]{:S(2)}) copy-start(s32[2,15]{1,0:T(2,128)} %param.106) | copy-start | bytes 364
  870.7 121.6 %all-reduce.42.cloned.1.call-start = ((), (), s32[]{:S(2)}) async-start(), calls=%async_computation.13 | async-start | bytes 786432 | tf_op jit(solution)/shard_map/psum | solution.py:29
  936.6 119.7 %all-reduce.44.cloned.1.call-start = ((), (), s32[]{:S(2)}) async-start(), calls=%async_computation.14 | async-start | bytes 786432 | tf_op jit(solution)/shard_map/psum | solution.py:74
  938.4 53.9 %copy-start.8 = (bf16[6,256,128]{1,2,0:T(8,128)(2,1)S(1)}, bf16[6,256,128]{1,2,0:T(8,128)(2,1)}, u32[]{:S(2)}) copy-start(bf16[6,256,128]{1,2,0:T(8,128)(2,1)} %broadcast_select_fusion.2) | copy-start | bytes 1179652
  995.1 127.0 %all-reduce.46.cloned.1.call-start = ((), (), s32[]{:S(2)}) async-start(), calls=%async_computation.15 | async-start | bytes 786432 | tf_op jit(solution)/shard_map/psum | solution.py:29
  1060.2 62.0 %copy-start.9 = (bf16[6,256,128]{1,2,0:T(8,128)(2,1)S(1)}, bf16[6,256,128]{1,2,0:T(8,128)(2,1)}, u32[]{:S(2)}) copy-start(bf16[6,256,128]{1,2,0:T(8,128)(2,1)} %broadcast_select_fusion.1) | copy-start | bytes 1179652
  1060.2 62.0 %copy-start.28 = (pred[6]{0:T(512)(128)(4,1)S(1)}, pred[6]{0:T(512)(128)(4,1)}, u32[]{:S(2)}) copy-start(pred[6]{0:T(512)(128)(4,1)} %get-tuple-element.900) | copy-start | bytes 22
  1060.2 124.5 %all-reduce.48.cloned.1.call-start = ((), (), s32[]{:S(2)}) async-start(), calls=%async_computation.16 | async-start | bytes 786432 | tf_op jit(solution)/shard_map/psum | solution.py:74
  1127.1 57.7 %copy-start.56 = (s32[2,15]{1,0:T(2,128)S(1)}, s32[2,15]{1,0:T(2,128)}, u32[]{:S(2)}) copy-start(s32[2,15]{1,0:T(2,128)} %param.106) | copy-start | bytes 364
  1128.0 111.2 %all-reduce.50.cloned.1.call-start = ((), (), s32[]{:S(2)}) async-start(), calls=%async_computation.17 | async-start | bytes 786432 | tf_op jit(solution)/shard_map/psum | solution.py:29
  1184.8 19.6 %copy-start.27 = (pred[6]{0:T(512)(128)(4,1)S(1)}, pred[6]{0:T(512)(128)(4,1)}, u32[]{:S(2)}) copy-start(pred[6]{0:T(512)(128)(4,1)} %get-tuple-element.753) | copy-start | bytes 22
  1205.2 98.3 %all-reduce.52.cloned.1.call-start = ((), (), s32[]{:S(2)}) async-start(), calls=%async_computation.18 | async-start | bytes 786432 | tf_op jit(solution)/shard_map/psum | solution.py:74
  1245.8 57.7 %copy-start.57 = (s32[2,15]{1,0:T(2,128)S(1)}, s32[2,15]{1,0:T(2,128)}, u32[]{:S(2)}) copy-start(s32[2,15]{1,0:T(2,128)} %param.106) | copy-start | bytes 364
  1320.6 2.4 copy-start.1
  (5 other events, 8.2 us)
Sparse Core Ops, SparseCore 0:
  11.6 54.0 all-reduce.19
  79.5 56.5 all-reduce.21
  152.4 54.1 all-reduce.23
  227.2 55.8 all-reduce.53
  307.4 113.4 reduce-scatter.1
  441.1 54.0 all-reduce.25
  499.9 58.7 all-reduce.27
  564.0 53.5 all-reduce.29
  622.4 59.6 all-reduce.31
  687.2 54.4 all-reduce.33
  746.5 59.7 all-reduce.35
  811.4 54.5 all-reduce.37
  870.8 60.4 all-reduce.39
  936.7 55.4 all-reduce.41
  995.8 60.5 all-reduce.43
  1060.3 61.7 all-reduce.45
  1128.2 56.5 all-reduce.47
  1205.4 33.8 all-reduce.49
  1246.9 56.5 all-reduce.51
where the time goes:
time: 1340 us; the launch traced here: 1330 us
  waiting for transfers between devices  1110 us (83%)
  matrix products  57.6 us (4%)
  local copies, waits for them, and re-layouts  56.4 us (4%)
  other arithmetic  51.8 us (4%)
  starting transfers between devices  20.1 us (2%)
  between operations  14.9 us (1%)
    psum x11, waiting for transfers between devices, column_sum(): lax.psum(partial_value.astype(jnp.bfloat16), 'col').astype(jnp.float32)  631 us
    psum x7, waiting for transfers between devices, from_root(): return lax.psum(kept, axis)  361 us
    reduce_scatter x1, waiting for transfers between devices, on_device(): lax.psum_scatter(dense, ('row', 'col'), scatter_dimension=0, tiled=True)  113 us
  transfers between devices with their start and end apart: 23, of which 23 were waited for; matrix products, arithmetic and copies ran while one was open for 1% of the time, Pallas kernels for 0%

commit v1 on v0

v1 whole, which is shorter than its diff:
```python
import functools

import jax
import jax.numpy as jnp
from jax import lax
from jax.experimental import pallas as pl
from jax.experimental.pallas import tpu as pltpu
from jax.sharding import PartitionSpec as P

MESH = pl.DeviceIdType.MESH
BF16 = jnp.bfloat16
F32 = jnp.float32


def dot_nt(a, b):
    return lax.dot_general(a, b, (((1,), (1,)), ((), ())), preferred_element_type=F32)


def dot_nn(a, b):
    return jnp.dot(a, b, preferred_element_type=F32)


def keep(coeffs, rank):
    lane = lax.broadcasted_iota(jnp.int32, coeffs.shape, 1)
    return jnp.where(lane < rank, coeffs, 0.0).astype(BF16)


def kernel(
    rows,
    cols,
    p_ranks, p_slots, in_ranks, c_ranks, c_slots, cin_ranks, b_ranks, b_inv,
    p_rhs, c_rhs,
    h_pinv, h_pl, h_pr, h_il, h_ir, h_cinv, h_cl, h_cr, h_cil, h_cir, h_bl, h_br,
    c_out, p_out,
    v_pinv, v_pl, v_pr, v_il, v_ir, v_cinv, v_cl, v_cr, v_cil, v_cir, v_bl, v_br,
    cx, px,
    cs, cf, ps, pf, bs, bf, bsum, zs, zf, side, acc,
    load_sem,
    cf_send, cf_recv, pf_send, pf_recv, bf_send, bf_recv, zf_send, zf_recv,
    cx_send, cx_recv, px_send, px_recv, cz_send, cz_recv, pz_send, pz_recv,
):
    row = lax.axis_index("row")
    col = lax.axis_index("col")
    half = rows // 2
    child = row // half
    place = row % half

    loads = [
        pltpu.make_async_copy(src, dst, load_sem.at[n])
        for n, (src, dst) in enumerate(
            (
                (h_cinv, v_cinv), (h_cir, v_cir), (h_cil, v_cil),
                (h_cr, v_cr), (h_cl, v_cl), (h_br, v_br), (h_bl, v_bl),
                (h_pinv, v_pinv), (h_ir, v_ir), (h_il, v_il),
                (h_pr, v_pr), (h_pl, v_pl),
            )
        )
    ]
    for load in loads:
        load.start()

    barrier = pltpu.get_barrier_semaphore()
    for d in range(1, cols):
        pl.semaphore_signal(
            barrier, inc=1, device_id=(row, lax.rem(col + d, cols)), device_id_type=MESH
        )
    for d in range(1, rows):
        pl.semaphore_signal(
            barrier, inc=1, device_id=(lax.rem(row + d, rows), col), device_id_type=MESH
        )
    pl.semaphore_wait(barrier, cols + rows - 2)

    def scatter_cols(sent, got, send_sem, recv_sem):
        copies = []
        for d in range(1, cols):
            peer = lax.rem(col + d, cols)
            copies.append(
                pltpu.make_async_remote_copy(
                    src_ref=sent.at[peer],
                    dst_ref=got.at[col],
                    send_sem=send_sem.at[d],
                    recv_sem=recv_sem.at[d],
                    device_id=(row, peer),
                    device_id_type=MESH,
                )
            )
        for copy in copies:
            copy.start()
        for copy in copies:
            copy.wait()

    def share_cols(x, first, count, send_sem, recv_sem):
        copies = []
        for d in range(1, cols):
            peer = lax.rem(col + d, cols)
            piece = x.at[pl.ds(first, count), col]
            copies.append(
                pltpu.make_async_remote_copy(
                    src_ref=piece,
                    dst_ref=piece,
                    send_sem=send_sem.at[d],
                    recv_sem=recv_sem.at[d],
                    device_id=(row, peer),
                    device_id_type=MESH,
                )
            )
        for copy in copies:
            copy.start()
        return copies

    def far_sums(x, first_row, group, limit, slots, ranks, v_r, v_l, out):
        nslots = v_r.shape[1]
        rmax, tile = v_r.shape[2], v_r.shape[3]
        for g in range(group):
            i = first_row + g
            parts = []
            for k in range(nslots):
                slot = slots(k)
                rank = ranks[i, k]
                if limit is not None:
                    rank = jnp.where(slot < limit, rank, 0)
                xk = x[slot].reshape(-1, tile)
                parts.append(keep(dot_nt(xk, v_r[i, k]), rank))
            coeffs = jnp.concatenate(parts, axis=1)
            total = dot_nn(coeffs, v_l[i].reshape(nslots * rmax, tile))
            out[:, g] = total.astype(BF16).reshape(cols, -1, tile)

    def chain(rhs, base, group, lb, v_inv, v_nr, v_nl, near_ranks, x, first):
        run = [acc[t] for t in range(group)]
        for t in range(group):
            y = dot_nt(run[t].astype(BF16), v_inv[base + t]).astype(BF16)
            x[first + t, col] = y
            for u in range(t + 1, group):
                p = u * (u - 1) // 2 + t
                coeffs = keep(dot_nt(y, v_nr[lb, p]), near_ranks[lb, p])
                run[u] = run[u] - dot_nn(coeffs, v_nl[lb, p])

    def solve(b, lb, group, x, rhs, slots, ranks, v_r, v_l, sent, got,
              send_sem, recv_sem, v_inv, v_nr, v_nl, near_ranks):
        base = lb * group
        first = b * group
        for g in range(group):
            acc[g] = rhs[base + g].astype(F32)

        @pl.when(b > 0)
        def _():
            far_sums(x, base, group, first, slots, ranks, v_r, v_l, sent.at[lb])
            scatter_cols(sent.at[lb], got.at[lb], send_sem, recv_sem.at[lb])
            for g in range(group):
                total = sent[lb, col, g].astype(F32)
                for d in range(1, cols):
                    total = total + got[lb, lax.rem(col + d, cols), g].astype(F32)
                acc[g] = acc[g] - total

        chain(rhs, base, group, lb, v_inv, v_nr, v_nl, near_ranks, x, first)

    c_blocks = v_cil.shape[0]
    c_group = v_cinv.shape[0] // c_blocks
    for load in loads[:5]:
        load.wait()

    @pl.loop(0, c_blocks * half)
    def _(b):
        owner = b // c_blocks
        lb = b % c_blocks
        first = b * c_group

        @pl.when(place == owner)
        def _():
            solve(b, lb, c_group, cx, c_rhs, lambda k: c_slots[child, k], c_ranks,
                  v_cr, v_cl, cs, cf, cf_send, cf_recv, v_cinv, v_cir, v_cil, cin_ranks)
            copies = []
            for d in range(1, half):
                peer = child * half + lax.rem(place + d, half)
                piece = cx.at[pl.ds(first, c_group), col]
                copies.append(
                    pltpu.make_async_remote_copy(
                        src_ref=piece, dst_ref=piece,
                        send_sem=cz_send.at[d], recv_sem=cz_recv.at[b],
                        device_id=(peer, col), device_id_type=MESH,
                    )
                )
            for copy in copies:
                copy.start()
            for copy in share_cols(cx, first, c_group, cx_send, cx_recv.at[b]):
                copy.wait()
            for copy in copies:
                copy.wait_send()

        @pl.when(place != owner)
        def _():
            piece = cx.at[pl.ds(first, c_group), col]
            pltpu.make_async_copy(piece, piece, cz_recv.at[b]).wait()
            for copy in share_cols(cx, first, c_group, cx_send, cx_recv.at[b]):
                copy.wait()

    for load in loads[5:7]:
        load.wait()
    n_border = v_bl.shape[0]
    far_sums(cx, 0, n_border, None, lambda k: c_slots[child, k], b_ranks, v_br, v_bl, bs)
    scatter_cols(bs, bf, bf_send, bf_recv)
    for k in range(n_border):
        total = bs[col, k].astype(F32)
        for d in range(1, cols):
            total = total + bf[lax.rem(col + d, cols), k].astype(F32)
        bsum[k] = total
    bsum[n_border] = jnp.zeros(bsum.shape[1:], F32)
    p_tiles = v_pinv.shape[0]
    copies = []
    for d in range(1, rows):
        peer = lax.rem(row + d, rows)
        for p in range(p_tiles):
            zs[d, p] = bsum[b_inv[peer * p_tiles + p]].astype(BF16)
        copies.append(
            pltpu.make_async_remote_copy(
                src_ref=zs.at[d], dst_ref=zf.at[d],
                send_sem=zf_send.at[d], recv_sem=zf_recv.at[d],
                device_id=(peer, col), device_id_type=MESH,
            )
        )
        copies[-1].start()
    c_tiles = v_cinv.shape[0]
    for t in range(c_tiles):
        c_out[t] = cx[place * c_tiles + t].reshape(c_out.shape[1:])
    for p in range(p_tiles):
        side[p] = p_rhs[p].astype(F32) - bsum[b_inv[row * p_tiles + p]]
    for copy in copies:
        copy.wait()
    for p in range(p_tiles):
        total = side[p]
        for d in range(1, rows):
            total = total - zf[d, p].astype(F32)
        side[p] = total

    p_blocks = v_il.shape[0]
    p_group = p_tiles // p_blocks
    for load in loads[7:]:
        load.wait()

    @pl.loop(0, p_blocks * rows)
    def _(b):
        owner = b // p_blocks
        lb = b % p_blocks
        first = b * p_group

        @pl.when(row == owner)
        def _():
            solve(b, lb, p_group, px, side, lambda k: p_slots[k], p_ranks,
                  v_pr, v_pl, ps, pf, pf_send, pf_recv, v_pinv, v_ir, v_il, in_ranks)
            piece = px.at[pl.ds(first, p_group), col]

            def below(d):
                return pltpu.make_async_remote_copy(
                    src_ref=piece, dst_ref=piece,
                    send_sem=pz_send.at[d], recv_sem=pz_recv.at[b],
                    device_id=(lax.rem(row + d, rows), col), device_id_type=MESH,
                )

            for d in range(1, rows):
                @pl.when(row + d < rows)
                def _():
                    below(d).start()
            for copy in share_cols(px, first, p_group, px_send, px_recv.at[b]):
                copy.wait()
            for d in range(1, rows):
                @pl.when(row + d < rows)
                def _():
                    below(d).wait_send()

        @pl.when(row > owner)
        def _():
            piece = px.at[pl.ds(first, p_group), col]
            pltpu.make_async_copy(piece, piece, pz_recv.at[b]).wait()
            for copy in share_cols(px, first, p_group, px_send, px_recv.at[b]):
                copy.wait()

    for t in range(p_tiles):
        p_out[t] = px[row * p_tiles + t].reshape(p_out.shape[1:])


def on_device(
    rows,
    cols,
    parent_rhs, parent_inverse, parent_left, parent_right, parent_ranks, parent_slots,
    inner_left, inner_right, inner_ranks,
    child_rhs, child_inverse, child_left, child_right, child_ranks, child_slots,
    child_inner_left, child_inner_right, child_inner_ranks,
    border_left, border_right, border_ranks, border_map,
):
    tile = parent_inverse.shape[1]
    nrhs = parent_rhs.shape[1]
    width = nrhs // cols
    col = lax.axis_index("col")
    p_tiles, c_tiles = parent_inverse.shape[0], child_inverse.shape[0]
    p_blocks, c_blocks = inner_left.shape[0], child_inner_left.shape[0]
    p_group, c_group = p_tiles // p_blocks, c_tiles // c_blocks
    n_border = border_left.shape[0]
    p_all = p_tiles * rows
    c_all = c_tiles * (rows // 2)

    def cut(rhs, tiles):
        mine = lax.dynamic_slice_in_dim(rhs, col * width, width, axis=1)
        return mine.reshape(tiles, tile, width).transpose(0, 2, 1)

    index = jnp.arange(n_border, dtype=jnp.int32)[:, None]
    hit = border_map[:, None] == jnp.arange(p_all, dtype=jnp.int32)[None, :]
    inverse_map = jnp.min(jnp.where(hit, index, n_border), axis=0)

    big = (
        parent_inverse, parent_left, parent_right, inner_left, inner_right,
        child_inverse, child_left, child_right, child_inner_left, child_inner_right,
        border_left, border_right,
    )
    smem = pl.BlockSpec(memory_space=pltpu.SMEM)
    vmem = pl.BlockSpec(memory_space=pltpu.VMEM)
    hbm = pl.BlockSpec(memory_space=pl.ANY)
    dma = pltpu.SemaphoreType.DMA
    c_out, p_out = pl.pallas_call(
        functools.partial(kernel, rows, cols),
        out_shape=(
            jax.ShapeDtypeStruct((c_tiles, nrhs, tile), BF16),
            jax.ShapeDtypeStruct((p_tiles, nrhs, tile), BF16),
        ),
        in_specs=[smem] * 8 + [vmem] * 2 + [hbm] * len(big),
        out_specs=(vmem, vmem),
        scratch_shapes=[pltpu.VMEM(a.shape, a.dtype) for a in big]
        + [
            pltpu.VMEM((c_all, cols, width, tile), BF16),
            pltpu.VMEM((p_all, cols, width, tile), BF16),
            pltpu.VMEM((c_blocks, cols, c_group, width, tile), BF16),
            pltpu.VMEM((c_blocks, cols, c_group, width, tile), BF16),
            pltpu.VMEM((p_blocks, cols, p_group, width, tile), BF16),
            pltpu.VMEM((p_blocks, cols, p_group, width, tile), BF16),
            pltpu.VMEM((cols, n_border, width, tile), BF16),
            pltpu.VMEM((cols, n_border, width, tile), BF16),
            pltpu.VMEM((n_border + 1, width, tile), F32),
            pltpu.VMEM((rows, p_tiles, width, tile), BF16),
            pltpu.VMEM((rows, p_tiles, width, tile), BF16),
            pltpu.VMEM((p_tiles, width, tile), F32),
            pltpu.VMEM((max(p_group, c_group), width, tile), F32),
            dma((len(big),)),
            dma((cols,)), dma((c_blocks, cols)),
            dma((cols,)), dma((p_blocks, cols)),
            dma((cols,)), dma((cols,)),
            dma((rows,)), dma((rows,)),
            dma((cols,)), dma((c_blocks * (rows // 2), cols)),
            dma((cols,)), dma((p_blocks * rows, cols)),
            dma((rows,)), dma((c_blocks * (rows // 2),)),
            dma((rows,)), dma((p_blocks * rows,)),
        ],
        compiler_params=pltpu.CompilerParams(
            collective_id=0, has_side_effects=True, vmem_limit_bytes=60 * 1024 * 1024
        ),
    )(
        parent_ranks, parent_slots, inner_ranks, child_ranks, child_slots,
        child_inner_ranks, border_ranks, inverse_map,
        cut(parent_rhs, p_tiles), cut(child_rhs, c_tiles),
        *big,
    )
    return (
        c_out.transpose(0, 2, 1).reshape(c_tiles * tile, nrhs),
        p_out.transpose(0, 2, 1).reshape(p_tiles * tile, nrhs),
    )


def solution(mesh):
    two, three, four = P("row", None), P("row", None, None), P("row", None, None, None)
    placed = (
        two, three, P("row", "col", None, None), P("row", "col", None, None),
        P("row", "col"), P("col"), four, four, two,
        two, three, P("row", "col", None, None), P("row", "col", None, None),
        P("row", "col"), P(None, "col"), four, four, two,
        P("row", "col", None, None), P("row", "col", None, None), P("row", "col"), P("row"),
    )
    return jax.shard_map(
        functools.partial(on_device, mesh.shape["row"], mesh.shape["col"]),
        mesh=mesh,
        in_specs=placed,
        out_specs=(two, two),
        check_vma=False,
    )
```

time: 1340 us -> 218 us (0.16)
  waiting for transfers between devices: 1110 us -> 0 us
  Pallas kernels: 0 us -> 205 us
  matrix products: 57.6 us -> 0 us
  other arithmetic: 51.8 us -> 1.33 us
  local copies, waits for them, and re-layouts: 56.4 us -> 11.6 us
  starting transfers between devices: 20.1 us -> 0 us
  between operations: 14.9 us -> 0.66 us
    psum x18 -> x0, waiting for transfers between devices: 992 us -> none  [the longest x11 631 us: column_sum(): lax.psum(partial_value.astype(jnp.bfloat16), 'col').astype(jnp.float32)]
    pallas_call x0 -> x1, Pallas kernels: none -> 205 us  [on_device(): pl.pallas_call(functools.partial(kernel, rows, cols), out_shape=(jax.Shap...]
    reduce_scatter x1 -> x0, waiting for transfers between devices: 113 us -> none  [on_device(): lax.psum_scatter(dense, ('row', 'col'), scatter_dimension=0, tiled=True)]
    dot_general x42 -> x0, matrix products: 57.6 us -> none  [the longest x20 19.9 us: solve_block(): jnp.dot(inverse[position], residue, preferred_element_type=jnp.float32)]
    select_n x24 -> x0, other arithmetic: 25.4 us -> none  [the longest x7 11.6 us: from_root(): jnp.where(lax.axis_index(axis) == source, value, 0).astype(value.dtype)]
    ppermute x4 -> x0, starting transfers between devices: 19.3 us -> none  [swapped(): return lax.ppermute(value, axis, pairs)]
    gather x11 -> x0, local copies, waits for them, and re-layouts: 17.1 us -> none  [the longest x7 14.9 us: on_device(): jnp.take(new_tiles, jnp.clip(parent_slots - step_index * GP, 0, GP - 1),...]
    cond x18 -> x0, local copies, waits for them, and re-layouts: 15.6 us -> none  [the longest x8 11.3 us: on_device(): lax.cond(is_owner, lambda: far_block(parent_left[lower:upper], parent_rig...]
  transfers between devices with their start and end apart: 23 -> 0, of which waited for: 23 -> 0; matrix products, arithmetic and copies ran while one was open for 1% -> 0% of each run, Pallas kernels for 0% -> 0%
where the time goes in v1:
time: 218 us
  Pallas kernels  205 us (94%)
  local copies, waits for them, and re-layouts  11.6 us (5%)
    pallas_call x1, Pallas kernels, on_device(): pl.pallas_call(functools.partial(kernel, rows, cols), out_shape=(jax.Shap...  205 us

profile of v1, /device:TPU:25, one launch (start us, length us, event | category | flops | bytes accessed | tf_op | source)
XLA Modules:
  0.0 218.1 jit_solution(3031786746825715342)
XLA Ops:
  0.6 0.0 copy-start
  0.6 1.3 select_reduce_fusion.b_inv
  2.0 1.3 copy.41.c_ranks
  3.3 1.3 copy.42.b_ranks
  4.7 1.4 copy.40.p_ranks
  6.0 1.2 constant_dynamic-slice_fusion
  7.3 0.8 copy.39
  8.1 0.0 copy-done
  8.1 0.3 constant_dynamic-slice_fusion.1
  8.4 0.9 copy.37
  9.3 204.5 %shard_map.221 = (bf16[8,128,256]{2,1,0:T(8,128)(2,1)}, bf16[12,128,256]{2,1,0:T(8,128)(2,1)}) custom-call(s32[12,6]{1,0:T(8,128)} %copy.40.p_ranks, s32[6]{0:T(128)} %p_slots.1, s32[2,15]{1,0:T(2,128)} %in_ranks.1, s32[8,2]{1,0:T(8,128)} %copy.41.c_ranks, s32[2,2]{1,0:T(2,128)} %c_slots.1, s32[2,6]{1,0:T(2,128)} %cin_ranks.1, s32[8,2]{1,0:T(8,128)} %copy.42.b_ranks, ...), custom_call_target="tpu_custom_call" | custom-call | tf_op jit(solution)/shard_map/pallas_call | solution.py:318
  213.8 2.0 copy.43
  215.8 2.3 %copy.44 = bf16[12,256,128]{2,1,0:T(8,128)(2,1)} copy(bf16[12,256,128]{1,2,0:T(8,128)(2,1)} %bitcast.11) | data formatting | bytes 1572864 | tf_op jit(solution)/shard_map/transpose | solution.py:362
Async XLA Ops:
  0.6 7.5 %copy-start = (bf16[3072,128]{1,0:T(8,128)(2,1)S(1)}, bf16[3072,128]{1,0:T(8,128)(2,1)}, u32[]{:S(2)}) copy-start(bf16[3072,128]{1,0:T(8,128)(2,1)} %param.22) | copy-start | bytes 2359300

commit v2 on v1

v2 whole, which is shorter than its diff:
```python
import functools
import math

import jax
import jax.numpy as jnp
from jax import lax
from jax.experimental import pallas as pl
from jax.experimental.pallas import tpu as pltpu
from jax.sharding import PartitionSpec as P

MESH = pl.DeviceIdType.MESH
BF16 = jnp.bfloat16
F32 = jnp.float32


def dot_nt(a, b):
    return lax.dot_general(a, b, (((1,), (1,)), ((), ())), preferred_element_type=F32)


def dot_nn(a, b):
    return jnp.dot(a, b, preferred_element_type=F32)


def keep(coeffs, rank):
    lane = lax.broadcasted_iota(jnp.int32, coeffs.shape, 1)
    return jnp.where(lane < rank, coeffs, 0.0).astype(BF16)


class View:
    def __init__(self, table, start, shape):
        self.table, self.start, self.shape = table, start, shape

    def __getitem__(self, at):
        if len(self.shape) == 1:
            return self.table[self.start + at]
        return self.table[self.start + at[0] * self.shape[1] + at[1]]


def views(table, shapes):
    start, found = 0, []
    for shape in shapes:
        found.append(View(table, start, shape))
        start += math.prod(shape)
    return found


def kernel(
    rows,
    cols,
    shapes,
    table,
    p_side, c_side,
    h_pinv, h_pl, h_pr, h_il, h_ir, h_cinv, h_cl, h_cr, h_cil, h_cir, h_bl, h_br,
    c_out, p_out,
    v_pinv, v_pl, v_pr, v_il, v_ir, v_cinv, v_cl, v_cr, v_cil, v_cir, v_bl, v_br,
    cx, px,
    cs, cf, ps, pf, bs, bf, bsum, zs, zf, side, known, p_rhs, c_rhs,
    load_sem,
    cf_send, cf_recv, pf_send, pf_recv, bf_send, bf_recv, zf_send, zf_recv,
    cx_send, cx_recv, px_send, px_recv, cz_send, cz_recv, pz_send, pz_recv,
):
    row = lax.axis_index("row")
    col = lax.axis_index("col")
    p_ranks, p_slots, in_ranks, c_ranks, c_slots, cin_ranks, b_ranks, b_inv = views(table, shapes)
    half = rows // 2
    child = row // half
    place = row % half

    loads = [
        pltpu.make_async_copy(src, dst, load_sem.at[n])
        for n, (src, dst) in enumerate(
            (
                (h_cinv, v_cinv), (h_cir, v_cir), (h_cil, v_cil),
                (h_cr, v_cr), (h_cl, v_cl), (h_br, v_br), (h_bl, v_bl),
                (h_pinv, v_pinv), (h_ir, v_ir), (h_il, v_il),
                (h_pr, v_pr), (h_pl, v_pl),
            )
        )
    ]
    for load in loads:
        load.start()

    barrier = pltpu.get_barrier_semaphore()
    for d in range(1, cols):
        pl.semaphore_signal(
            barrier, inc=1, device_id=(row, lax.rem(col + d, cols)), device_id_type=MESH
        )
    for d in range(1, rows):
        pl.semaphore_signal(
            barrier, inc=1, device_id=(lax.rem(row + d, rows), col), device_id_type=MESH
        )
    pl.semaphore_wait(barrier, cols + rows - 2)

    tile = c_side.shape[0] // v_cinv.shape[0]
    for side_in, turned in ((c_side, c_rhs), (p_side, p_rhs)):
        for n in range(turned.shape[0]):
            turned[n] = side_in[n * tile:(n + 1) * tile].T.reshape(turned.shape[1:])

    def scatter_tile(sent, got, g, send_sem, recv_sem):
        copies = []
        for d in range(1, cols):
            peer = lax.rem(col + d, cols)
            copies.append(
                pltpu.make_async_remote_copy(
                    src_ref=sent.at[peer, g],
                    dst_ref=got.at[col, g],
                    send_sem=send_sem.at[g, d],
                    recv_sem=recv_sem.at[g, d],
                    device_id=(row, peer),
                    device_id_type=MESH,
                )
            )
        return copies

    def gathered(sent, got, g):
        total = sent[col, g].astype(F32)
        for d in range(1, cols):
            total = total + got[lax.rem(col + d, cols), g].astype(F32)
        return total

    def share_cols(piece, send_sem, recv_sem):
        copies = []
        for d in range(1, cols):
            copies.append(
                pltpu.make_async_remote_copy(
                    src_ref=piece,
                    dst_ref=piece,
                    send_sem=send_sem.at[d],
                    recv_sem=recv_sem.at[d],
                    device_id=(row, lax.rem(col + d, cols)),
                    device_id_type=MESH,
                )
            )
        return copies

    def far_sums(x, first_row, group, limit, slots, ranks, v_r, v_l, sent, got, send_sem, recv_sem):
        nslots = v_r.shape[1]
        rmax, tile = v_r.shape[2], v_r.shape[3]
        for k in range(nslots):
            known[k] = x[slots(k)].reshape(known.shape[1:])
        for g in range(group):
            i = first_row + g
            parts = []
            for k in range(nslots):
                rank = ranks[i, k]
                if limit is not None:
                    rank = jnp.where(slots(k) < limit, rank, 0)
                parts.append(keep(dot_nt(known[k], v_r[i, k]), rank))
            coeffs = jnp.concatenate(parts, axis=1)
            total = dot_nn(coeffs, v_l[i].reshape(nslots * rmax, tile))
            sent[:, g] = total.astype(BF16).reshape(cols, -1, tile)
            for copy in scatter_tile(sent, got, g, send_sem, recv_sem):
                copy.start()

    def solve(b, lb, group, x, rhs, slots, ranks, v_r, v_l, sent, got,
              send_sem, recv_sem, v_inv, v_nr, v_nl, near_ranks, after, far):
        base = lb * group
        first = b * group
        if far:
            far_sums(x, base, group, first, slots, ranks, v_r, v_l,
                     sent.at[lb], got.at[lb], send_sem, recv_sem.at[lb])
        near = [None] * group
        for t in range(group):
            residue = rhs(base + t).astype(F32)
            if near[t] is not None:
                residue = residue - near[t]
            if far:
                for copy in scatter_tile(sent.at[lb], got.at[lb], t, send_sem, recv_sem.at[lb]):
                    copy.wait()
                residue = residue - gathered(sent.at[lb], got.at[lb], t)
            y = dot_nt(residue.astype(BF16), v_inv[base + t]).astype(BF16)
            x[first + t, col] = y
            after(first + t)
            for u in range(t + 1, group):
                p = u * (u - 1) // 2 + t
                coeffs = keep(dot_nt(y, v_nr[lb, p]), near_ranks[lb, p])
                part = dot_nn(coeffs, v_nl[lb, p])
                near[u] = part if near[u] is None else near[u] + part

    def front(steps, blocks, group, place, peers, reaches, x, z_send, z_recv, x_send, x_recv, solver):
        def step(b, far):
            owner = b // blocks
            lb = b % blocks
            first = b * group
            whole = x.at[pl.ds(first, group), col]

            def across(piece, t, d):
                return pltpu.make_async_remote_copy(
                    src_ref=piece, dst_ref=piece,
                    send_sem=z_send.at[d], recv_sem=z_recv.at[b, t],
                    device_id=(peers(d), col), device_id_type=MESH,
                )

            def each_peer(act):
                for d in range(1, steps // blocks):
                    pl.when(reaches(d))(functools.partial(act, d))

            @pl.when(place == owner)
            def _():
                def after(tile):
                    piece = x.at[tile, col]
                    each_peer(lambda d: across(piece, tile - first, d).start())
                    for copy in share_cols(piece, x_send, x_recv.at[b]):
                        copy.start()

                solver(b, lb, after, far)
                for copy in share_cols(whole, x_send, x_recv.at[b]):
                    copy.wait()
                each_peer(lambda d: across(whole, 0, d).wait_send())

            @pl.when(takes(owner))
            def _():
                for t in range(group):
                    piece = x.at[first + t, col]
                    pltpu.make_async_copy(piece, piece, z_recv.at[b, t]).wait()
                    for copy in share_cols(piece, x_send, x_recv.at[b]):
                        copy.start()
                for copy in share_cols(whole, x_send, x_recv.at[b]):
                    copy.wait()

        if reaches is always:
            takes = lambda owner: place != owner
        else:
            takes = lambda owner: place > owner
        step(0, False)
        pl.loop(1, steps)(lambda b: step(b, True))

    always = lambda d: d > 0

    c_blocks = v_cil.shape[0]
    c_group = v_cinv.shape[0] // c_blocks
    for load in loads[:5]:
        load.wait()

    def child_solver(b, lb, after, far):
        solve(b, lb, c_group, cx, lambda n: c_rhs[n, col], lambda k: c_slots[child, k], c_ranks, v_cr, v_cl,
              cs, cf, cf_send, cf_recv, v_cinv, v_cir, v_cil, cin_ranks, after, far)

    front(c_blocks * half, c_blocks, c_group, place,
          lambda d: child * half + lax.rem(place + d, half), always,
          cx, cz_send, cz_recv, cx_send, cx_recv, child_solver)

    for load in loads[5:7]:
        load.wait()
    n_border = v_bl.shape[0]
    far_sums(cx, 0, n_border, None, lambda k: c_slots[child, k], b_ranks, v_br, v_bl,
             bs, bf, bf_send, bf_recv)
    for k in range(n_border):
        for copy in scatter_tile(bs, bf, k, bf_send, bf_recv):
            copy.wait()
        bsum[k] = gathered(bs, bf, k)
    bsum[n_border] = jnp.zeros(bsum.shape[1:], F32)
    p_tiles = v_pinv.shape[0]
    p_blocks = v_il.shape[0]
    p_group = p_tiles // p_blocks

    def lifted(q, l):
        return pltpu.make_async_remote_copy(
            src_ref=zs.at[q, l], dst_ref=zf.at[row, l],
            send_sem=zf_send.at[q, l], recv_sem=zf_recv.at[row, l],
            device_id=(q, col), device_id_type=MESH,
        )

    for q in range(rows):
        @pl.when(row != q)
        def _():
            for l in range(p_blocks):
                for g in range(p_group):
                    p = (q * p_blocks + l) * p_group + g
                    zs[q, l, g] = bsum[b_inv[p]].astype(BF16)
                lifted(q, l).start()

    for p in range(p_tiles):
        side[p] = p_rhs[p, col].astype(F32) - bsum[b_inv[row * p_tiles + p]]
    c_tiles = v_cinv.shape[0]
    for t in range(c_tiles):
        c_out[t] = cx[place * c_tiles + t].reshape(c_out.shape[1:])

    for load in loads[7:]:
        load.wait()

    def parent_solver(b, lb, after, far):
        for d in range(1, rows):
            q = lax.rem(row + d, rows)
            arrived = zf.at[q, lb]
            pltpu.make_async_copy(arrived, arrived, zf_recv.at[q, lb]).wait()
        for g in range(p_group):
            total = side[lb * p_group + g]
            for d in range(1, rows):
                total = total - zf[lax.rem(row + d, rows), lb, g].astype(F32)
            side[lb * p_group + g] = total
        solve(b, lb, p_group, px, lambda n: side[n], lambda k: p_slots[k], p_ranks, v_pr, v_pl,
              ps, pf, pf_send, pf_recv, v_pinv, v_ir, v_il, in_ranks, after, far)

    front(p_blocks * rows, p_blocks, p_group, row,
          lambda d: lax.rem(row + d, rows), lambda d: row + d < rows,
          px, pz_send, pz_recv, px_send, px_recv, parent_solver)

    for q in range(rows):
        @pl.when(row != q)
        def _():
            for l in range(p_blocks):
                lifted(q, l).wait_send()

    for t in range(p_tiles):
        p_out[t] = px[row * p_tiles + t].reshape(p_out.shape[1:])


def on_device(
    rows,
    cols,
    parent_rhs, parent_inverse, parent_left, parent_right, parent_ranks, parent_slots,
    inner_left, inner_right, inner_ranks,
    child_rhs, child_inverse, child_left, child_right, child_ranks, child_slots,
    child_inner_left, child_inner_right, child_inner_ranks,
    border_left, border_right, border_ranks, border_map,
):
    tile = parent_inverse.shape[1]
    nrhs = parent_rhs.shape[1]
    width = nrhs // cols
    p_tiles, c_tiles = parent_inverse.shape[0], child_inverse.shape[0]
    p_blocks, c_blocks = inner_left.shape[0], child_inner_left.shape[0]
    p_group, c_group = p_tiles // p_blocks, c_tiles // c_blocks
    n_border = border_left.shape[0]
    p_all = p_tiles * rows
    c_all = c_tiles * (rows // 2)

    index = jnp.arange(n_border, dtype=jnp.int32)[:, None]
    hit = border_map[:, None] == jnp.arange(p_all, dtype=jnp.int32)[None, :]
    inverse_map = jnp.min(jnp.where(hit, index, n_border), axis=0)

    numbers = (
        parent_ranks, parent_slots, inner_ranks, child_ranks, child_slots,
        child_inner_ranks, border_ranks, inverse_map,
    )
    big = (
        parent_inverse, parent_left, parent_right, inner_left, inner_right,
        child_inverse, child_left, child_right, child_inner_left, child_inner_right,
        border_left, border_right,
    )
    smem = pl.BlockSpec(memory_space=pltpu.SMEM)
    vmem = pl.BlockSpec(memory_space=pltpu.VMEM)
    hbm = pl.BlockSpec(memory_space=pl.ANY)
    dma = pltpu.SemaphoreType.DMA
    c_out, p_out = pl.pallas_call(
        functools.partial(kernel, rows, cols, tuple(a.shape for a in numbers)),
        out_shape=(
            jax.ShapeDtypeStruct((c_tiles, nrhs, tile), BF16),
            jax.ShapeDtypeStruct((p_tiles, nrhs, tile), BF16),
        ),
        in_specs=[smem] + [vmem] * 2 + [hbm] * len(big),
        out_specs=(vmem, vmem),
        scratch_shapes=[pltpu.VMEM(a.shape, a.dtype) for a in big]
        + [
            pltpu.VMEM((c_all, cols, width, tile), BF16),
            pltpu.VMEM((p_all, cols, width, tile), BF16),
            pltpu.VMEM((c_blocks, cols, c_group, width, tile), BF16),
            pltpu.VMEM((c_blocks, cols, c_group, width, tile), BF16),
            pltpu.VMEM((p_blocks, cols, p_group, width, tile), BF16),
            pltpu.VMEM((p_blocks, cols, p_group, width, tile), BF16),
            pltpu.VMEM((cols, n_border, width, tile), BF16),
            pltpu.VMEM((cols, n_border, width, tile), BF16),
            pltpu.VMEM((n_border + 1, width, tile), F32),
            pltpu.VMEM((rows, p_blocks, p_group, width, tile), BF16),
            pltpu.VMEM((rows, p_blocks, p_group, width, tile), BF16),
            pltpu.VMEM((p_tiles, width, tile), F32),
            pltpu.VMEM((max(parent_left.shape[1], child_left.shape[1]), nrhs, tile), BF16),
            pltpu.VMEM((p_tiles, cols, width, tile), BF16),
            pltpu.VMEM((c_tiles, cols, width, tile), BF16),
            dma((len(big),)),
            dma((c_group, cols)), dma((c_blocks, c_group, cols)),
            dma((p_group, cols)), dma((p_blocks, p_group, cols)),
            dma((n_border, cols)), dma((n_border, cols)),
            dma((rows, p_blocks)), dma((rows, p_blocks)),
            dma((cols,)), dma((c_blocks * (rows // 2), cols)),
            dma((cols,)), dma((p_blocks * rows, cols)),
            dma((rows,)), dma((c_blocks * (rows // 2), c_group)),
            dma((rows,)), dma((p_blocks * rows, p_group)),
        ],
        compiler_params=pltpu.CompilerParams(
            collective_id=0, has_side_effects=True, vmem_limit_bytes=60 * 1024 * 1024
        ),
    )(
        jnp.concatenate([a.reshape(-1) for a in numbers]),
        parent_rhs, child_rhs,
        *big,
    )
    return (
        c_out.transpose(0, 2, 1).reshape(c_tiles * tile, nrhs),
        p_out.transpose(0, 2, 1).reshape(p_tiles * tile, nrhs),
    )


def solution(mesh):
    two, three, four = P("row", None), P("row", None, None), P("row", None, None, None)
    placed = (
        two, three, P("row", "col", None, None), P("row", "col", None, None),
        P("row", "col"), P("col"), four, four, two,
        two, three, P("row", "col", None, None), P("row", "col", None, None),
        P("row", "col"), P(None, "col"), four, four, two,
        P("row", "col", None, None), P("row", "col", None, None), P("row", "col"), P("row"),
    )
    return jax.shard_map(
        functools.partial(on_device, mesh.shape["row"], mesh.shape["col"]),
        mesh=mesh,
        in_specs=placed,
        out_specs=(two, two),
        check_vma=False,
    )
```

time: 218 us -> 166 us (0.76)
  Pallas kernels: 205 us -> 153 us
    pallas_call x1, Pallas kernels: 205 us -> 153 us  [on_device(): pl.pallas_call(functools.partial(kernel, rows, cols, tuple((a.shape for a...]
where the time goes in v2:
time: 166 us; the launch traced here: 165 us
  Pallas kernels  153 us (92%)
  local copies, waits for them, and re-layouts  10.4 us (6%)
    pallas_call x1, Pallas kernels, on_device(): pl.pallas_call(functools.partial(kernel, rows, cols, tuple((a.shape for a...  153 us

profile of v2, /device:TPU:25, one launch (start us, length us, event | category | flops | bytes accessed | tf_op | source)
XLA Modules:
  0.0 165.2 jit_solution(10323903099890046135)
XLA Ops:
  0.6 0.8 reshape.30
  1.4 0.8 reshape.32
  2.1 0.8 reshape.33
  2.9 0.7 select_reduce_fusion
  3.6 0.8 copy.33
  4.4 0.1 reshape.31
  4.5 0.8 copy.34
  5.2 0.1 reshape.34
  5.3 0.8 copy.32
  6.1 0.1 reshape.29
  6.2 1.3 concatenate.3.table
  7.5 153.4 %shard_map.221 = (bf16[8,128,256]{2,1,0:T(8,128)(2,1)}, bf16[12,128,256]{2,1,0:T(8,128)(2,1)}) custom-call(s32[204]{0:T(256)} %concatenate.3.table, bf16[3072,128]{1,0:T(8,128)(2,1)} %p_side.1, bf16[2048,128]{1,0:T(8,128)(2,1)} %c_side.1, bf16[12,256,256]{2,1,0:T(8,128)(2,1)} %h_pinv.1, bf16[12,6,128,256]{3,2,1,0:T(8,128)(2,1)} %h_pl.1, ...), custom_call_target="tpu_custom_call" | custom-call | tf_op jit(solution)/shard_map/pallas_call | solution.py:345
  160.9 2.0 %copy.35 = bf16[8,256,128]{2,1,0:T(8,128)(2,1)} copy(bf16[8,256,128]{1,2,0:T(8,128)(2,1)} %bitcast.7) | data formatting | bytes 1048576 | tf_op jit(solution)/shard_map/transpose | solution.py:389
  162.9 2.3 %copy.36 = bf16[12,256,128]{2,1,0:T(8,128)(2,1)} copy(bf16[12,256,128]{1,2,0:T(8,128)(2,1)} %bitcast.5) | data formatting | bytes 1572864 | tf_op jit(solution)/shard_map/transpose | solution.py:390
